TPU v7x, 32 devices: a whole 2x2x4 slice. The times are simulated.
32 devices in a mesh: row: 4 (over x, core), col: 8 (over z, y).
Axes of the slice: x: 2, y: 2, z: 4, core: 2. Of those that a mesh axis runs over, the one named last changes fastest.
Arguments:
- right_sides: float32 [3, 4, 512, 64], P(None, None, 'row'), may hold values from -6 to 6
- diag_inverse: float32 [3, 4, 512, 512], replicated, as said below
- sub_blocks: float32 [3, 4, 4, 512, 512], P(None, None, None, 'row', 'col'), may hold values from -0.125 to 0.125
- block_mask: int32 [3, 4, 4], replicated, may hold values 0 or 1
- anc_values: float32 [2, 4, 512, 512], P(None, None, 'row', 'col'), may hold values from -0.09375 to 0.09375
- anc_rows: int32 [2, 4, 512], P(None, None, 'row'), may hold values from 0 to 2047, as said below
- anc_count: int32 [2, 4], replicated, may hold values from 256 to 512, as said below
- far_factor: float32 [4, 512, 32768], P(None, 'col', 'row'), may hold values from -0.1875 to 0.1875
- far_rhs: float32 [32768, 64], P(('row', 'col')), may hold values from -6 to 6
- far_solution: float32 [32768, 64], P('row'), may hold values from -4 to 4
Outputs:
- forward_solution: float32 [3, 4, 512, 64], P(None, None, 'row')
- solution: float32 [3, 4, 512, 64], P(None, None, 'row')
- far_update: float32 [32768, 64], P(('row', 'col'))
Inputs may be any that keep to these rules, and one draw needn't show every extreme that they name: `diag_inverse`: each diagonal-block inverse is lower triangular. `anc_rows`: each list holds distinct rows of the parent's window in ascending order; entries at positions anc_count or later are not used. `anc_count`: some list is full and some holds exactly 256 live entries in every draw. `block_mask`: entries on and above the block diagonal are not used.
All inputs are finite; a program needn't handle non-finite values.
Results may differ from a plain program's by a relative error of at most 0.0001.
Values sent between devices are 32-bit elements; how exact they have to be, the bound alone decides.
A program may use at most 128 MiB of HBM per device.

v0:
```python
import jax
import jax.numpy as jnp
from jax import lax
from jax.sharding import PartitionSpec as P

FULL_PRECISION = lax.Precision.HIGHEST


def strict_lower(length):
    positions = jnp.arange(length)
    return (positions[:, None] > positions[None, :]).astype(jnp.float32)


def whole_forward(right_whole, inverse, lower_blocks, weights, extra, pair_of):
    panels = right_whole.shape[1]
    solved = []
    for panel_index in range(panels):
        residual = right_whole[:, panel_index] - extra[:, panel_index]
        for earlier in range(panel_index):
            block = lower_blocks[:, pair_of[panel_index, earlier]]
            term = jnp.einsum("bij,bjk->bik", block, solved[earlier], precision=FULL_PRECISION)
            residual = residual - term * weights[:, panel_index, earlier][:, None, None]
        solved.append(
            jnp.einsum("bij,bjk->bik", inverse[:, panel_index], residual, precision=FULL_PRECISION)
        )
    return jnp.stack(solved, axis=1)


def whole_backward(forward, inverse, lower_blocks, weights, extra, pair_of):
    panels = forward.shape[1]
    solved = [None] * panels
    for panel_index in reversed(range(panels)):
        residual = forward[:, panel_index] - extra[:, panel_index]
        for later in range(panel_index + 1, panels):
            block = lower_blocks[:, pair_of[later, panel_index]]
            term = jnp.einsum("bij,bik->bjk", block, solved[later], precision=FULL_PRECISION)
            residual = residual - term * weights[:, later, panel_index][:, None, None]
        solved[panel_index] = jnp.einsum(
            "bji,bjk->bik", inverse[:, panel_index], residual, precision=FULL_PRECISION
        )
    return jnp.stack(solved, axis=1)


def place_columns(local_term, col_start, width):
    shape = local_term.shape[:-2] + (width, local_term.shape[-1])
    return lax.dynamic_update_slice_in_dim(
        jnp.zeros(shape, jnp.float32), local_term, col_start, local_term.ndim - 2
    )


def on_device(
    right_sides,
    diag_inverse,
    sub_blocks,
    block_mask,
    anc_values,
    anc_rows,
    anc_count,
    far_factor,
    far_rhs,
    far_solution,
):
    row_width = right_sides.shape[2]
    col_width = sub_blocks.shape[4]
    columns = right_sides.shape[3]
    panels = diag_inverse.shape[1]
    width = diag_inverse.shape[2]
    row_start = lax.axis_index("row") * row_width
    col_start = lax.axis_index("col") * col_width
    kept_blocks = block_mask.astype(jnp.float32) * strict_lower(panels)[None]
    anc_width = anc_rows.shape[2]
    position = lax.axis_index("row") * anc_width + jnp.arange(anc_width)
    live_rows = (position[None, None, :] < anc_count[:, :, None]).astype(jnp.float32)
    pair_list_rows = [later for later in range(panels) for earlier in range(later)]
    pair_list_cols = [earlier for later in range(panels) for earlier in range(later)]
    pair_of = {}
    for pair_index in range(len(pair_list_rows)):
        pair_of[pair_list_rows[pair_index], pair_list_cols[pair_index]] = pair_index
    pair_rows = jnp.array(pair_list_rows, dtype=jnp.int32)
    pair_cols = jnp.array(pair_list_cols, dtype=jnp.int32)
    lower_local = sub_blocks[:, pair_rows, pair_cols]
    lower_part = lax.all_gather(lower_local, "row", axis=2, tiled=True)
    lower_blocks = lax.all_gather(lower_part, "col", axis=3, tiled=True)
    right_whole = lax.all_gather(right_sides, "row", axis=2, tiled=True)
    zero_extra = jnp.zeros((2, panels, width, columns), jnp.float32)
    child_forward = whole_forward(
        right_whole[:2], diag_inverse[:2], lower_blocks[:2], kept_blocks[:2], zero_extra, pair_of
    )
    child_cols = lax.dynamic_slice_in_dim(child_forward, col_start, col_width, 2)
    updates = jnp.einsum("spaj,spjk->spak", anc_values, child_cols, precision=FULL_PRECISION)
    updates = updates * live_rows[..., None]
    spread = (
        jnp.zeros((panels * width, columns), jnp.float32)
        .at[anc_rows.reshape(-1)]
        .add(updates.reshape(-1, columns))
    )
    ancestor = lax.psum(spread, ("row", "col")).reshape(panels, width, columns)
    parent_forward = whole_forward(
        right_whole[2:],
        diag_inverse[2:],
        lower_blocks[2:],
        kept_blocks[2:],
        ancestor[None],
        pair_of,
    )
    parent_cols = lax.dynamic_slice_in_dim(parent_forward[0], col_start, col_width, 1)
    far_update = far_rhs - lax.psum_scatter(
        jnp.einsum("pjr,pjk->rk", far_factor, parent_cols, precision=FULL_PRECISION),
        "col",
        scatter_dimension=0,
        tiled=True,
    )
    far_back = jnp.einsum("pjr,rk->pjk", far_factor, far_solution, precision=FULL_PRECISION)
    far_whole = lax.psum(place_columns(far_back, col_start, width), ("row", "col"))
    parent_solution = whole_backward(
        parent_forward,
        diag_inverse[2:],
        lower_blocks[2:],
        kept_blocks[2:],
        far_whole[None],
        pair_of,
    )
    parent_flat = parent_solution[0].reshape(panels * width, columns)
    picked = parent_flat[anc_rows] * live_rows[..., None]
    child_extra = jnp.einsum("spaj,spak->spjk", anc_values, picked, precision=FULL_PRECISION)
    extra_whole = lax.psum(place_columns(child_extra, col_start, width), ("row", "col"))
    child_solution = whole_backward(
        child_forward, diag_inverse[:2], lower_blocks[:2], kept_blocks[:2], extra_whole, pair_of
    )
    forward_all = jnp.concatenate([child_forward, parent_forward], axis=0)
    solution_all = jnp.concatenate([child_solution, parent_solution], axis=0)
    forward_rows = lax.dynamic_slice_in_dim(forward_all, row_start, row_width, 2)
    solution_rows = lax.dynamic_slice_in_dim(solution_all, row_start, row_width, 2)
    return (forward_rows, solution_rows, far_update)


def solution(mesh):
    in_specs = (
        P(None, None, "row", None),
        P(),
        P(None, None, None, "row", "col"),
        P(),
        P(None, None, "row", "col"),
        P(None, None, "row"),
        P(),
        P(None, "col", "row"),
        P(("row", "col"), None),
        P("row", None),
    )
    out_specs = (P(None, None, "row", None), P(None, None, "row", None), P(("row", "col"), None))
    return jax.shard_map(
        on_device, mesh=mesh, in_specs=in_specs, out_specs=out_specs, check_vma=False
    )
```

profile of v0, /device:TPU:1, one launch (start us, length us, event | category | flops | bytes accessed | tf_op | source)
XLA Modules:
  0.0 857.3 jit_solution(2775651494124286492)
XLA Ops:
  7.2 3.1 gather_fusion
  12.3 25.1 %all-gather.6.cloned.1.call-done = f32[3,6,512,64]{2,3,0,1:T(8,128)} async-done(((f32[3,6,128,64]{2,3,0,1:T(8,128)}), f32[3,6,512,64]{2,3,0,1:T(8,128)}) %all-gather.6.cloned.1.call-update) | async-done | bytes 2359312 | tf_op jit(solution)/shard_map/all_gather | solution.py:82
  37.4 3.3 copy.100
  41.6 14.5 %fusion.66 = f32[1,4,64,64]{2,3,1,0:T(8,128)S(1)} fusion(f32[4,64,8192]{2,1,0:T(8,128)} %param.19, f32[8192,64]{0,1:T(8,128)S(1)} %copy-done), kind=kOutput, calls=%fused_computation.86 | convolution fusion | flops 1610612736 | bytes 10551296 | tf_op jit(solution)/shard_map/pjr,rk->pjk/dot_general | solution.py:113
  57.4 2.0 all-gather.4.cloned.1.call-done
  59.4 3.7 fusion.14
  63.1 359.9 %all-gather.8.cloned.1.call-done = f32[3,6,512,512]{2,3,1,0:T(8,128)} async-done(((f32[3,6,512,64]{2,3,1,0:T(8,128)}), f32[3,6,512,512]{2,3,1,0:T(8,128)}) %all-gather.8.cloned.1.call-update) | async-done | bytes 18874384 | tf_op jit(solution)/shard_map/all_gather | solution.py:83
  423.0 3.1 fusion.59
  426.1 3.7 fusion.10
  429.8 3.0 fusion.55
  432.8 3.0 fusion.51
  435.9 3.7 fusion.6
  439.6 3.0 fusion.47
  442.6 3.0 fusion.43
  445.7 3.2 fusion.39
  448.9 3.7 fusion.2
  453.3 6.3 scatter_custom_fusion
  461.5 128.7 %all-reduce.6.cloned.1.call-done = (f32[1,4,512,64]{2,3,1,0:T(8,128)}, f32[1,4,512,64]{2,3,1,0:T(8,128)}) async-done(((f32[1,4,512,64]{2,3,1,0:T(8,128)}, f32[1,4,512,64]{2,3,1,0:T(8,128)}), (f32[1,4,512,64]{2,3,1,0:T(8,128)}, f32[1,4,512,64]{2,3,1,0:T(8,128)})) %all-reduce.6.cloned.1.call-update) | async-done | bytes 1048592 | tf_op jit(solution)/shard_map/psum | solution.py:97
  590.1 2.5 fusion.94
  592.6 2.7 fusion.69
  595.4 2.3 fusion.91
  597.7 2.6 convolution_multiply_fusion.10
  600.3 2.7 fusion.71
  603.1 2.3 fusion.87
  605.4 2.6 convolution_multiply_fusion.8
  608.0 2.7 convolution_multiply_fusion.7
  610.7 2.7 fusion.74
  613.4 2.3 fusion.83
  617.8 3.0 fusion.75
  622.7 3.0 convolution_multiply_fusion.4
  625.7 3.0 fusion.77
  630.7 3.4 convolution_multiply_fusion.1
  634.1 3.0 convolution_multiply_fusion.2
  637.1 3.0 fusion.80
  643.4 2.8 gather_fusion.1
  649.6 8.9 %convolution_bitcast_fusion = f32[8192,64]{0,1:T(8,128)} fusion(f32[4,64,8192]{2,1,0:T(8,128)} %param.19, f32[1,4,512,64]{2,3,1,0:T(8,128)S(1)} %get-tuple-element.26, s32[]{:T(128)S(6)} %select_n.32), kind=kOutput, calls=%fused_computation.3 | convolution fusion | flops 1610612736 | bytes 10616836 | tf_op jit(solution)/shard_map/pjr,pjk->rk/dot_general | solution.py:108
  658.6 120.2 %all-reduce.4.cloned.1.call-done = f32[2,4,512,64]{2,3,0,1:T(8,128)} async-done(((f32[2,4,512,64]{2,3,0,1:T(8,128)}), f32[2,4,512,64]{2,3,0,1:T(8,128)}) %all-reduce.4.cloned.1.call-update) | async-done | bytes 1048592 | tf_op jit(solution)/shard_map/psum | solution.py:126
  778.8 3.1 fusion
  781.9 3.8 fusion.41
  785.8 3.1 fusion.4
  788.9 3.9 fusion.53
  792.8 3.8 fusion.45
  796.6 3.0 fusion.8
  799.6 3.8 fusion.61
  803.4 3.8 fusion.57
  807.2 3.8 fusion.49
  811.0 3.0 fusion.62
  815.7 32.9 %reduce-scatter.2.cloned.1.call-done = f32[1024,64]{0,1:T(8,128)} async-done(((f32[8192,64]{0,1:T(8,128)}), f32[1024,64]{0,1:T(8,128)}) %reduce-scatter.2.cloned.1.call-update) | async-done | bytes 262160 | tf_op jit(solution)/shard_map/reduce_scatter | solution.py:107
  (81 shorter events, 22.4 us)
Async XLA Ops:
  7.2 34.4 %copy-start = (f32[8192,64]{0,1:T(8,128)S(1)}, f32[8192,64]{0,1:T(8,128)}, u32[]{:S(2)}) copy-start(f32[8192,64]{0,1:T(8,128)} %param.21) | copy-start | bytes 6291460
  7.2 49.9 %copy-start.10 = (s32[3,4,4]{2,1,0:T(4,128)S(1)}, s32[3,4,4]{2,1,0:T(4,128)}, u32[]{:S(2)}) copy-start(s32[3,4,4]{2,1,0:T(4,128)} %param.15) | copy-start | bytes 580
  7.2 50.1 %copy-start.9 = (s32[2,4,128]{2,1,0:T(4,128)S(1)}, s32[2,4,128]{2,1,0:T(4,128)}, u32[]{:S(2)}) copy-start(s32[2,4,128]{2,1,0:T(4,128)} %param.17) | copy-start | bytes 12292
  7.2 30.2 %all-gather.6.cloned.1.call-start = ((), (), s32[]{:S(2)}) async-start(), calls=%async_computation.2 | async-start | bytes 2949120 | tf_op jit(solution)/shard_map/all_gather | solution.py:82
  10.4 49.0 %all-gather.4.cloned.1.call-start = ((), (), s32[]{:S(2)}) async-start(), calls=%async_computation.1 | async-start | bytes 1966080 | tf_op jit(solution)/shard_map/all_gather | solution.py:84
  12.2 410.8 %all-gather.8.cloned.1.call-start = ((), (), s32[]{:S(2)}) async-start(), calls=%async_computation.3 | async-start | bytes 21233664 | tf_op jit(solution)/shard_map/all_gather | solution.py:83
  40.7 549.4 %all-reduce.6.cloned.1.call-start = ((), (), s32[]{:S(2)}) async-start(), calls=%async_computation.6 | async-start | bytes 2097152 | tf_op jit(solution)/shard_map/psum | solution.py:97
  57.1 391.8 %copy-start.5 = (f32[1,4,512,64]{2,3,1,0:T(8,128)}, f32[1,4,512,64]{2,3,1,0:T(8,128)S(1)}, u32[]{:S(2)}) copy-start(f32[1,4,512,64]{2,3,1,0:T(8,128)S(1)} %dynamic_update_slice.8) | copy-start | bytes 1572868
  57.3 391.6 %copy-start.11 = (f32[2]{0:T(128)}, f32[2]{0:T(128)S(1)}, u32[]{:S(2)}) copy-start(f32[2]{0:T(128)S(1)} %get-tuple-element.19) | copy-start | bytes 28
  57.3 391.6 %copy-start.13 = (f32[2]{0:T(128)}, f32[2]{0:T(128)S(1)}, u32[]{:S(2)}) copy-start(f32[2]{0:T(128)S(1)} %get-tuple-element.23) | copy-start | bytes 28
  57.3 391.6 %copy-start.15 = (f32[2]{0:T(128)}, f32[2]{0:T(128)S(1)}, u32[]{:S(2)}) copy-start(f32[2]{0:T(128)S(1)} %get-tuple-element.21) | copy-start | bytes 28
  57.3 391.6 %copy-start.17 = (f32[2]{0:T(128)}, f32[2]{0:T(128)S(1)}, u32[]{:S(2)}) copy-start(f32[2]{0:T(128)S(1)} %get-tuple-element.18) | copy-start | bytes 28
  423.0 29.6 %copy-start.6 = (f32[2,4,128,64]{2,3,1,0:T(8,128)S(1)}, f32[2,4,128,64]{2,3,1,0:T(8,128)}, u32[]{:S(2)}) copy-start(f32[2,4,128,64]{2,3,1,0:T(8,128)} %param.16) | copy-start | bytes 786436
  460.8 318.0 %all-reduce.4.cloned.1.call-start = ((), (), s32[]{:S(2)}) async-start(), calls=%async_computation.4 | async-start | bytes 2097152 | tf_op jit(solution)/shard_map/psum | solution.py:126
  590.1 25.7 %copy-start.7 = (f32[1,4,512,64]{2,3,1,0:T(8,128)S(1)}, f32[1,4,512,64]{2,3,1,0:T(8,128)}, u32[]{:S(2)}) copy-start(f32[1,4,512,64]{2,3,1,0:T(8,128)} %get-tuple-element.25) | copy-start | bytes 1572868
  643.4 138.5 %copy-start.18 = (f32[2]{0:T(128)S(1)}, f32[2]{0:T(128)}, u32[]{:S(2)}) copy-start(f32[2]{0:T(128)} %copy-done.17) | copy-start | bytes 28
  646.9 142.0 %copy-start.16 = (f32[2]{0:T(128)S(1)}, f32[2]{0:T(128)}, u32[]{:S(2)}) copy-start(f32[2]{0:T(128)} %copy-done.15) | copy-start | bytes 28
  647.6 1.0 copy-start.2
  648.7 199.9 %reduce-scatter.2.cloned.1.call-start = ((), (), s32[]{:S(2)}) async-start(), calls=%async_computation.5 | async-start | bytes 2359296 | tf_op jit(solution)/shard_map/reduce_scatter | solution.py:107
  649.6 143.2 %copy-start.12 = (f32[2]{0:T(128)S(1)}, f32[2]{0:T(128)}, u32[]{:S(2)}) copy-start(f32[2]{0:T(128)} %copy-done.11) | copy-start | bytes 28
  649.6 150.0 %copy-start.14 = (f32[2]{0:T(128)S(1)}, f32[2]{0:T(128)}, u32[]{:S(2)}) copy-start(f32[2]{0:T(128)} %copy-done.13) | copy-start | bytes 28
  781.9 32.1 %copy-start.3 = (f32[1,4,512,64]{2,3,0,1:T(8,128)S(1)}, f32[1,4,512,64]{2,3,0,1:T(8,128)}, u32[]{:S(2)}) copy-start(f32[1,4,512,64]{2,3,0,1:T(8,128)} %get-tuple-element.28) | copy-start | bytes 1572868
  781.9 32.1 %copy-start.4 = (f32[1,4,512,64]{2,3,0,1:T(8,128)S(1)}, f32[1,4,512,64]{2,3,0,1:T(8,128)}, u32[]{:S(2)}) copy-start(f32[1,4,512,64]{2,3,0,1:T(8,128)} %get-tuple-element.27) | copy-start | bytes 1572868
  785.7 64.5 %copy-start.1 = (f32[8192,64]{0,1:T(8,128)S(1)}, f32[8192,64]{0,1:T(8,128)}, u32[]{:S(2)}) copy-start(f32[8192,64]{0,1:T(8,128)} %param.21) | copy-start | bytes 6291460
  788.9 59.7 %copy-start.8 = (f32[1024,64]{0,1:T(8,128)S(1)}, f32[1024,64]{0,1:T(8,128)}, u32[]{:S(2)}) copy-start(f32[1024,64]{0,1:T(8,128)} %param.20) | copy-start | bytes 786436
Sparse Core Ops, SparseCore 0:
  10.5 26.8 all-gather.5
  39.5 19.8 all-gather.3
  60.9 362.0 all-gather.7
  460.9 129.1 all-reduce.5
  648.8 129.9 all-reduce.3
  782.2 66.3 reduce-scatter.1
where the time goes:
time: 866 us; the launch traced here: 857 us
  waiting for transfers between devices  669 us (77%)
  matrix products  145 us (17%)
  local copies, waits for them, and re-layouts  18 us (2%)
  between operations  14.7 us (2%)
  other arithmetic  10.7 us (1%)
    all_gather x1, waiting for transfers between devices, on_device(): lower_blocks = lax.all_gather(lower_part, 'col', axis=3, tiled=True)  360 us
    psum x1, waiting for transfers between devices, on_device(): ancestor = lax.psum(spread, ('row', 'col')).reshape(panels, width, columns)  129 us
    psum x1, waiting for transfers between devices, on_device(): lax.psum(place_columns(child_extra, col_start, width), ('row', 'col'))  120 us
    dot_general x12, matrix products, whole_backward(): jnp.einsum('bij,bik->bjk', block, solved[later], precision=FULL_PRECISION)  41.2 us
    dot_general x12, matrix products, whole_forward(): jnp.einsum('bij,bjk->bik', block, solved[earlier], precision=FULL_PRECISION)  34.6 us
    reduce_scatter x1, waiting for transfers between devices, on_device(): lax.psum_scatter(jnp.einsum('pjr,pjk->rk', far_factor, parent_cols, preci...  32.9 us
    all_gather x1, waiting for transfers between devices, on_device(): lower_part = lax.all_gather(lower_local, 'row', axis=2, tiled=True)  25.1 us
    dot_general x8, matrix products, whole_forward(): jnp.einsum('bij,bjk->bik', inverse[:, panel_index], residual, precision=F...  24.4 us
  transfers between devices with their start and end apart: 6, of which 6 were waited for; matrix products, arithmetic and copies ran while one was open for 8% of the time, Pallas kernels for 0%

commit v1 on v0

v1 whole, which is shorter than its diff:
```python
import functools

import jax
import jax.numpy as jnp
from jax import lax
from jax.experimental import pallas as pl
from jax.experimental.pallas import tpu as pltpu
from jax.sharding import PartitionSpec as P

MESH = pl.DeviceIdType.MESH
NN = (((1,), (0,)), ((), ()))
NT = (((1,), (1,)), ((), ()))
VMEM_LIMIT = 56 * 1024 * 1024


def halves(value):
    high = value.astype(jnp.bfloat16)
    low = (value - high.astype(jnp.float32)).astype(jnp.bfloat16)
    return high, low


def product(left, right, dims):
    left_high, left_low = halves(left)
    right_high, right_low = halves(right)
    rows = left.shape[0]
    both = lax.dot_general(
        jnp.concatenate([left_high, left_low], axis=0),
        right_high,
        dims,
        preferred_element_type=jnp.float32,
    )
    cross = lax.dot_general(left_high, right_low, dims, preferred_element_type=jnp.float32)
    return both[:rows] + (both[rows:] + cross)


def selected(left, choice, dims):
    high, low = halves(left)
    least = (left - high.astype(jnp.float32) - low.astype(jnp.float32)).astype(jnp.bfloat16)
    rows = left.shape[0]
    stacked = lax.dot_general(
        jnp.concatenate([high, low, least], axis=0),
        choice,
        dims,
        preferred_element_type=jnp.float32,
    )
    return stacked[:rows] + (stacked[rows : 2 * rows] + stacked[2 * rows :])


def enter(peers, me):
    barrier = pltpu.get_barrier_semaphore()
    for offset in range(1, peers):
        pl.semaphore_signal(
            barrier,
            inc=1,
            device_id={"row": lax.rem(me + offset, peers)},
            device_id_type=MESH,
        )
    pl.semaphore_wait(barrier, peers - 1)


def send_all(source_of, landing, send_sems, recv_sems, step, peers, me):
    copies = []
    for offset in range(1, peers):
        dest = lax.rem(me + offset, peers)
        copy = pltpu.make_async_remote_copy(
            src_ref=source_of(dest),
            dst_ref=landing,
            send_sem=send_sems.at[step, offset],
            recv_sem=recv_sems.at[step, offset],
            device_id={"row": dest},
            device_id_type=MESH,
        )
        copy.start()
        copies.append(copy)
    return copies


def pair_table(panels):
    pairs = [(later, earlier) for later in range(panels) for earlier in range(later)]
    return {pair: index for index, pair in enumerate(pairs)}, pairs


def tile_of(ref, index, lanes):
    value = ref[:, index, :, 0:lanes]
    return value.reshape(value.shape[0] * value.shape[1], lanes)


def forward_kernel(
    peers,
    panels,
    right_ref,
    inverse_ref,
    child_ref,
    parent_ref,
    choice_ref,
    slices_ref,
    whole_ref,
    gathered,
    parts,
    arrived,
    send_sems,
    recv_sems,
):
    me = lax.axis_index("row")
    pair_of, pairs = pair_table(panels)
    count = len(pairs)
    rows = right_ref.shape[3]
    enter(peers, me)
    started = []

    def spread(step, separators):
        copies = send_all(
            lambda dest: gathered.at[step, me, pl.ds(0, separators)],
            gathered.at[step, me, pl.ds(0, separators)],
            send_sems,
            recv_sems,
            step,
            peers,
            me,
        )
        for copy in copies:
            copy.wait_recv()
        started.extend(copies)
        return [
            jnp.concatenate([gathered[step, peer, index] for peer in range(peers)], axis=1)
            for index in range(separators)
        ]

    solved = [[], []]
    for panel in range(panels):
        for child in range(2):
            residual = right_ref[child, panel]
            for earlier in range(panel):
                tile = tile_of(child_ref, child * count + pair_of[panel, earlier], rows)
                residual = residual - product(solved[child][earlier], tile, NN)
            gathered[panel, me, child] = residual
        whole = spread(panel, 2)
        for child in range(2):
            value = product(whole[child], inverse_ref[child, panel], NT)
            solved[child].append(value)
            for peer in range(peers):
                parts[peer, :, 0:rows] = value[:, peer * rows : (peer + 1) * rows]
            slices_ref[child, panel] = parts[me, :, 0:rows]
    updates = []
    for child in range(2):
        for panel in range(panels):
            tile = tile_of(child_ref, 2 * count + child * panels + panel, child_ref.shape[3])
            updates.append(product(solved[child][panel], tile, NN))
    update = selected(jnp.concatenate(updates, axis=1), choice_ref[...], NN)
    width = peers * rows
    for peer in range(peers):
        for panel in range(panels):
            begin = panel * width + peer * rows
            parts[peer, :, panel * rows : (panel + 1) * rows] = update[:, begin : begin + rows]
    step = 2 * panels
    copies = send_all(
        lambda dest: parts.at[dest], arrived.at[me], send_sems, recv_sems, step, peers, me
    )
    for copy in copies:
        copy.wait_recv()
    started.extend(copies)
    ancestor = parts[me]
    for offset in range(1, peers):
        ancestor = ancestor + arrived[lax.rem(me + offset, peers)]
    solved = []
    for panel in range(panels):
        residual = right_ref[2, panel] - ancestor[:, panel * rows : (panel + 1) * rows]
        for earlier in range(panel):
            tile = tile_of(parent_ref, pair_of[panel, earlier], rows)
            residual = residual - product(solved[earlier], tile, NN)
        gathered[panels + panel, me, 0] = residual
        whole = spread(panels + panel, 1)
        value = product(whole[0], inverse_ref[2, panel], NT)
        solved.append(value)
        whole_ref[panel] = value
    for copy in started:
        copy.wait_send()
    for panel in range(panels):
        for peer in range(peers):
            parts[peer, :, 0:rows] = solved[panel][:, peer * rows : (peer + 1) * rows]
        slices_ref[2, panel] = parts[me, :, 0:rows]


def backward_kernel(
    peers,
    panels,
    forward_ref,
    inverse_ref,
    child_ref,
    parent_ref,
    choice_ref,
    far_ref,
    slices_ref,
    gathered,
    parts,
    arrived,
    mine,
    send_sems,
    recv_sems,
):
    me = lax.axis_index("row")
    pair_of, pairs = pair_table(panels)
    count = len(pairs)
    rows = forward_ref.shape[3]
    enter(peers, me)
    started = []

    def summed(step, forward, partials):
        separators = len(partials)
        for index in range(separators):
            for peer in range(peers):
                parts[step, peer, index] = partials[index][:, peer * rows : (peer + 1) * rows]
        copies = send_all(
            lambda dest: parts.at[step, dest, pl.ds(0, separators)],
            arrived.at[step, me, pl.ds(0, separators)],
            send_sems,
            recv_sems,
            2 * step,
            peers,
            me,
        )
        for copy in copies:
            copy.wait_recv()
        started.extend(copies)
        for index in range(separators):
            total = parts[step, me, index]
            for offset in range(1, peers):
                total = total + arrived[step, lax.rem(me + offset, peers), index]
            gathered[step, me, index] = forward[index] - total
        copies = send_all(
            lambda dest: gathered.at[step, me, pl.ds(0, separators)],
            gathered.at[step, me, pl.ds(0, separators)],
            send_sems,
            recv_sems,
            2 * step + 1,
            peers,
            me,
        )
        for copy in copies:
            copy.wait_recv()
        started.extend(copies)
        return [
            jnp.concatenate([gathered[step, peer, index] for peer in range(peers)], axis=1)
            for index in range(separators)
        ]

    def my_slice(value):
        for peer in range(peers):
            mine[peer] = value[:, peer * rows : (peer + 1) * rows]
        return mine[me]

    solved = [None] * panels
    own = [None] * panels
    for panel in reversed(range(panels)):
        partial = far_ref[panel]
        for later in range(panel + 1, panels):
            tile = tile_of(parent_ref, pair_of[later, panel], rows)
            partial = partial + product(own[later], tile, NT)
        step = panels - 1 - panel
        whole = summed(step, [forward_ref[2, panel]], [partial])
        solved[panel] = product(whole[0], inverse_ref[2, panel], NN)
        own[panel] = my_slice(solved[panel])
        slices_ref[2, panel] = own[panel]
    picked = selected(jnp.concatenate(solved, axis=1), choice_ref[...], NT)
    slots = choice_ref.shape[0] // (2 * panels)
    own = [[None] * panels, [None] * panels]
    for panel in reversed(range(panels)):
        partials = []
        for child in range(2):
            place = child * panels + panel
            tile = tile_of(child_ref, 2 * count + place, slots)
            partial = product(picked[:, place * slots : (place + 1) * slots], tile, NT)
            for later in range(panel + 1, panels):
                tile = tile_of(child_ref, child * count + pair_of[later, panel], rows)
                partial = partial + product(own[child][later], tile, NT)
            partials.append(partial)
        step = 2 * panels - 1 - panel
        whole = summed(step, [forward_ref[child, panel] for child in range(2)], partials)
        for child in range(2):
            value = product(whole[child], inverse_ref[child, panel], NN)
            own[child][panel] = my_slice(value)
            slices_ref[child, panel] = own[child][panel]
    for copy in started:
        copy.wait_send()


def on_device(
    peers,
    right_sides,
    diag_inverse,
    sub_blocks,
    block_mask,
    anc_values,
    anc_rows,
    anc_count,
    far_factor,
    far_rhs,
    far_solution,
):
    panels = diag_inverse.shape[1]
    width = diag_inverse.shape[2]
    rows = right_sides.shape[2]
    columns = right_sides.shape[3]
    col_width = sub_blocks.shape[4]
    slots = anc_rows.shape[2]
    _, pairs = pair_table(panels)
    vmem = pl.BlockSpec(memory_space=pltpu.VMEM)

    def lower(separator):
        tiles = [
            jnp.where(block_mask[separator, later, earlier] == 1, sub_blocks[separator, later, earlier], 0.0).T
            for later, earlier in pairs
        ]
        return tiles

    anc_tiles = anc_values.transpose(0, 1, 3, 2).reshape(2 * panels, col_width, slots)
    child_tiles = jnp.stack(lower(0) + lower(1))
    parent_tiles = jnp.stack(lower(2))
    if rows < slots:
        child_tiles = jnp.pad(child_tiles, ((0, 0), (0, 0), (0, slots - rows)))
    child_all = lax.all_gather(jnp.concatenate([child_tiles, anc_tiles]), "col")
    parent_all = lax.all_gather(parent_tiles, "col")

    position = lax.axis_index("row") * slots + jnp.arange(slots)
    live = position[None, None, :] < anc_count[:, :, None]
    wanted = jnp.where(live, anc_rows, -1).reshape(-1)
    choice = (wanted[:, None] == jnp.arange(panels * width)[None, :]).astype(jnp.bfloat16)

    far_back = jnp.einsum(
        "rk,pjr->pkj", far_solution, far_factor, precision=lax.Precision.HIGH
    )
    far_all = lax.all_gather(far_back, "col", axis=0)
    far_whole = far_all.transpose(1, 2, 0, 3).reshape(panels, columns, width)

    right_turned = right_sides.transpose(0, 1, 3, 2)
    slices, whole = pl.pallas_call(
        functools.partial(forward_kernel, peers, panels),
        out_shape=(
            jax.ShapeDtypeStruct((3, panels, columns, rows), jnp.float32),
            jax.ShapeDtypeStruct((panels, columns, width), jnp.float32),
        ),
        in_specs=[vmem] * 5,
        out_specs=(vmem, vmem),
        scratch_shapes=[
            pltpu.VMEM((2 * panels, peers, 2, columns, rows), jnp.float32),
            pltpu.VMEM((peers, columns, panels * rows), jnp.float32),
            pltpu.VMEM((peers, columns, panels * rows), jnp.float32),
            pltpu.SemaphoreType.DMA((2 * panels + 1, peers)),
            pltpu.SemaphoreType.DMA((2 * panels + 1, peers)),
        ],
        compiler_params=pltpu.CompilerParams(
            collective_id=0, has_side_effects=True, vmem_limit_bytes=VMEM_LIMIT
        ),
        name="forward",
    )(right_turned, diag_inverse, child_all, parent_all, choice)

    start = lax.axis_index("col") * col_width
    parent_cols = lax.dynamic_slice_in_dim(whole, start, col_width, 2)
    far_update = far_rhs - lax.psum_scatter(
        jnp.einsum("pjr,pkj->rk", far_factor, parent_cols, precision=lax.Precision.HIGH),
        "col",
        scatter_dimension=0,
        tiled=True,
    )

    turned = pl.pallas_call(
        functools.partial(backward_kernel, peers, panels),
        out_shape=jax.ShapeDtypeStruct((3, panels, columns, rows), jnp.float32),
        in_specs=[vmem] * 6,
        out_specs=vmem,
        scratch_shapes=[
            pltpu.VMEM((2 * panels, peers, 2, columns, rows), jnp.float32),
            pltpu.VMEM((2 * panels, peers, 2, columns, rows), jnp.float32),
            pltpu.VMEM((2 * panels, peers, 2, columns, rows), jnp.float32),
            pltpu.VMEM((peers, columns, rows), jnp.float32),
            pltpu.SemaphoreType.DMA((4 * panels, peers)),
            pltpu.SemaphoreType.DMA((4 * panels, peers)),
        ],
        compiler_params=pltpu.CompilerParams(
            collective_id=1, has_side_effects=True, vmem_limit_bytes=VMEM_LIMIT
        ),
        name="backward",
    )(slices, diag_inverse, child_all, parent_all, choice, far_whole)
    return (slices.transpose(0, 1, 3, 2), turned.transpose(0, 1, 3, 2), far_update)


def solution(mesh):
    in_specs = (
        P(None, None, "row", None),
        P(),
        P(None, None, None, "row", "col"),
        P(),
        P(None, None, "row", "col"),
        P(None, None, "row"),
        P(),
        P(None, "col", "row"),
        P(("row", "col"), None),
        P("row", None),
    )
    out_specs = (P(None, None, "row", None), P(None, None, "row", None), P(("row", "col"), None))
    return jax.shard_map(
        functools.partial(on_device, mesh.shape["row"]),
        mesh=mesh,
        in_specs=in_specs,
        out_specs=out_specs,
        check_vma=False,
    )
```

time: 866 us -> 361 us (0.42)
  waiting for transfers between devices: 669 us -> 128 us
  Pallas kernels: 0 us -> 140 us
  matrix products: 145 us -> 13.4 us
  blocking collectives: 0 us -> 30.6 us
  between operations: 14.7 us -> 25.3 us
  local copies, waits for them, and re-layouts: 18 us -> 8.44 us
    all_gather x3 -> x2, waiting for transfers between devices: 387 us -> 128 us  [the longest x1 87 us: on_device(): child_all = lax.all_gather(jnp.concatenate([child_tiles, anc_tiles]), 'col')]
    psum x2 -> x0, waiting for transfers between devices: 249 us -> none  [the longest x1 129 us: on_device(): ancestor = lax.psum(spread, ('row', 'col')).reshape(panels, width, columns)]
    pallas_call x0 -> x2, Pallas kernels: none -> 140 us  [the longest x1 84.3 us: on_device(): pl.pallas_call(functools.partial(backward_kernel, peers, panels), out_sha...]
    dot_general x44 -> x2, matrix products: 145 us -> 13.4 us  [the longest x1 7.61 us: on_device(): jnp.einsum('pjr,pkj->rk', far_factor, parent_cols, precision=lax.Precisio...]
    reduce_scatter x1, waiting for transfers between devices: 32.9 us -> 0.02 us  [on_device(): lax.psum_scatter(jnp.einsum('pjr,pkj->rk', far_factor, parent_cols, preci...]
    all_gather x0 -> x1, blocking collectives: none -> 30.6 us  [on_device(): far_all = lax.all_gather(far_back, 'col', axis=0)]
  transfers between devices with their start and end apart: 6 -> 3, of which waited for: 6 -> 2; matrix products, arithmetic and copies ran while one was open for 8% -> 3% of each run, Pallas kernels for 0% -> 23%
where the time goes in v1:
time: 361 us; the launch traced here: 359 us
  Pallas kernels  140 us (39%)
  waiting for transfers between devices  128 us (35%)
  blocking collectives  30.6 us (8%)
  between operations  25.3 us (7%)
  other arithmetic  13.8 us (4%)
  matrix products  13.4 us (4%)
  local copies, waits for them, and re-layouts  8.44 us (2%)
    all_gather x1, waiting for transfers between devices, on_device(): child_all = lax.all_gather(jnp.concatenate([child_tiles, anc_tiles]), 'col')  87 us
    pallas_call x1, Pallas kernels, on_device(): pl.pallas_call(functools.partial(backward_kernel, peers, panels), out_sha...  84.3 us
    pallas_call x1, Pallas kernels, on_device(): pl.pallas_call(functools.partial(forward_kernel, peers, panels), out_shap...  55.2 us
    all_gather x1, waiting for transfers between devices, on_device(): parent_all = lax.all_gather(parent_tiles, 'col')  41 us
    all_gather x1, blocking collectives, on_device(): far_all = lax.all_gather(far_back, 'col', axis=0)  30.6 us
    unnamed x11, other arithmetic  8.48 us
    dot_general x1, matrix products, on_device(): jnp.einsum('pjr,pkj->rk', far_factor, parent_cols, precision=lax.Precisio...  7.61 us
  transfers between devices with their start and end apart: 3, of which 2 were waited for; matrix products, arithmetic and copies ran while one was open for 3% of the time, Pallas kernels for 23%

profile of v1, /device:TPU:1, one launch (start us, length us, event | category | flops | bytes accessed | tf_op | source)
XLA Modules:
  0.0 359.4 jit_solution(14256176597850789129)
XLA Ops:
  7.2 0.0 copy-start
  7.2 0.0 copy-start.6
  7.2 0.0 copy-start.5
  7.2 0.0 all-gather.8.cloned.1.call-start
  7.2 1.6 fusion.8
  20.3 0.8 constant_dynamic-update-slice_fusion.12
  21.1 0.8 constant_dynamic-update-slice_fusion.11
  21.9 0.8 constant_dynamic-update-slice_fusion.10
  22.6 0.8 constant_dynamic-update-slice_fusion.9
  23.4 0.8 constant_dynamic-update-slice_fusion.8
  24.1 0.8 constant_dynamic-update-slice_fusion.7
  24.9 0.8 constant_dynamic-update-slice_fusion.18
  25.7 0.8 constant_dynamic-update-slice_fusion.17
  26.5 0.8 constant_dynamic-update-slice_fusion.16
  27.3 0.8 constant_dynamic-update-slice_fusion.15
  28.0 0.8 constant_dynamic-update-slice_fusion.14
  28.8 0.8 constant_dynamic-update-slice_fusion.13
  29.6 0.0 copy-start.3
  29.6 0.7 copy-done.3
  30.3 0.0 all-gather.8.cloned.1.call-update
  30.3 0.0 all-gather.6.cloned.1.call-start
  30.4 1.0 constant_dynamic-update-slice_fusion
  31.3 0.0 copy-start.2
  31.3 0.8 copy-done.2
  32.2 0.0 all-gather.6.cloned.1.call-update
  32.2 0.0 reduce-scatter.2.cloned.1.call-start
  32.2 0.0 copy-done.6
  32.3 0.0 copy-done.5
  32.3 0.1 compare_select_fusion
  32.3 2.8 fusion.choice_ref
  35.1 41.0 %all-gather.8.cloned.1.call-done = f32[48,64,128]{2,1,0:T(8,128)} async-done(((f32[6,64,128]{2,1,0:T(8,128)}), f32[48,64,128]{2,1,0:T(8,128)}) %all-gather.8.cloned.1.call-update) | async-done | bytes 1572880 | tf_op jit(solution)/shard_map/all_gather | solution.py:322
  76.2 87.0 %all-gather.6.cloned.1.call-done = f32[160,64,128]{2,1,0:T(8,128)} async-done(((f32[20,64,128]{2,1,0:T(8,128)}), f32[160,64,128]{2,1,0:T(8,128)}) %all-gather.6.cloned.1.call-update) | async-done | bytes 5242896 | tf_op jit(solution)/shard_map/all_gather | solution.py:321
  163.2 55.2 %forward.1 = (f32[3,4,64,128]{3,2,1,0:T(8,128)}, f32[4,64,512]{2,1,0:T(8,128)}) custom-call(f32[3,4,64,128]{3,2,1,0:T(8,128)} %bitcast.162, f32[3,4,512,512]{3,2,1,0:T(8,128)} %inverse_ref.3, f32[8,20,64,128]{3,2,1,0:T(8,128)} %bitcast.154, f32[8,6,64,128]{3,2,1,0:T(8,128)} %bitcast.156, bf16[1024,2048]{1,0:T(8,128)(2,1)} %fusion.choice_ref), custom_call_target="tpu_custom_call" | custom-call | tf_op jit(solution)/shard_map/forward/pallas_call | solution.py:336
  218.4 7.6 %convolution_bitcast_fusion = f32[8192,64]{0,1:T(8,128)} fusion(f32[4,64,8192]{2,1,0:T(8,128)} %param.17, f32[4,64,512]{2,1,0:T(8,128)} %get-tuple-element.6, s32[]{:T(128)S(6)} %select_n.226), kind=kOutput, calls=%fused_computation | convolution fusion | flops 805306368 | bytes 10616836 | tf_op jit(solution)/shard_map/pjr,pkj->rk/dot_general | solution.py:360
  226.1 0.0 reduce-scatter.2.cloned.1.call-update
  226.1 0.0 copy-done
  226.1 5.8 %fusion.3 = f32[4,64,64]{1,2,0:T(8,128)S(1)} fusion(f32[4,64,8192]{2,1,0:T(8,128)} %param.17, f32[8192,64]{0,1:T(8,128)S(1)} %copy-done), kind=kOutput, calls=%fused_computation.5 | convolution fusion | flops 805306368 | bytes 10551296 | tf_op jit(solution)/shard_map/rk,pjr->pkj/dot_general | solution.py:329
  231.9 0.1 copy.14
  232.0 30.6 %all-gather.2 = f32[32,64,64]{2,1,0:T(8,128)S(1)} all-gather(f32[4,64,64]{2,1,0:T(8,128)S(1)} %copy.14), channel_id=4, replica_groups=mesh['row'=4,'col'=8] {'col'}, dimensions={0}, use_global_device_ids=true | all-gather | bytes 589824 | tf_op jit(solution)/shard_map/all_gather | solution.py:332
  262.6 0.6 copy.17
  263.2 1.1 reshape.109.far_ref
  264.3 84.3 %backward.1 = f32[3,4,64,128]{3,2,1,0:T(8,128)} custom-call(f32[3,4,64,128]{3,2,1,0:T(8,128)} %get-tuple-element.5.forward_ref, f32[3,4,512,512]{3,2,1,0:T(8,128)} %inverse_ref.3, f32[8,20,64,128]{3,2,1,0:T(8,128)} %bitcast.155, f32[8,6,64,128]{3,2,1,0:T(8,128)} %bitcast.157, bf16[1024,2048]{1,0:T(8,128)(2,1)} %fusion.choice_ref, f32[4,64,512]{2,1,0:T(8,128)} %reshape.109.far_ref), custom_call_target="tpu_custom_call" | custom-call | tf_op jit(solution)/shard_map/backward/pallas_call | solution.py:366
  348.7 0.0 reduce-scatter.2.cloned.1.call-done
  348.7 0.0 copy-done.4
  348.7 1.7 sub.3
  350.4 0.0 copy-done.1
  350.4 0.7 copy.37
  351.1 1.8 copy.38
  (3 shorter events, 0.0 us)
Async XLA Ops:
  7.2 218.9 %copy-start = (f32[8192,64]{0,1:T(8,128)S(1)}, f32[8192,64]{0,1:T(8,128)}, u32[]{:S(2)}) copy-start(f32[8192,64]{0,1:T(8,128)} %param.19) | copy-start | bytes 6291460
  7.2 25.1 %copy-start.6 = (s32[2,4]{1,0:T(2,128)S(1)}, s32[2,4]{1,0:T(2,128)}, u32[]{:S(2)}) copy-start(s32[2,4]{1,0:T(2,128)} %param.16) | copy-start | bytes 100
  7.2 25.1 %copy-start.5 = (s32[2,4,128]{2,1,0:T(4,128)S(1)}, s32[2,4,128]{2,1,0:T(4,128)}, u32[]{:S(2)}) copy-start(s32[2,4,128]{2,1,0:T(4,128)} %param.15) | copy-start | bytes 12292
  7.2 69.0 %all-gather.8.cloned.1.call-start = ((), (), s32[]{:S(2)}) async-start(), calls=%async_computation.3 | async-start | bytes 1769472 | tf_op jit(solution)/shard_map/all_gather | solution.py:322
  29.6 0.7 copy-start.3
  30.3 132.9 %all-gather.6.cloned.1.call-start = ((), (), s32[]{:S(2)}) async-start(), calls=%async_computation.2 | async-start | bytes 5898240 | tf_op jit(solution)/shard_map/all_gather | solution.py:321
  31.3 0.8 copy-start.2
  32.2 316.5 %reduce-scatter.2.cloned.1.call-start = ((), (), s32[]{:S(2)}) async-start(), calls=%async_computation.1 | async-start | bytes 2359296 | tf_op jit(solution)/shard_map/reduce_scatter | solution.py:359
  264.3 84.4 %copy-start.4 = (f32[1024,64]{0,1:T(8,128)S(1)}, f32[1024,64]{0,1:T(8,128)}, u32[]{:S(2)}) copy-start(f32[1024,64]{0,1:T(8,128)} %param.18) | copy-start | bytes 786436
  264.3 86.1 %copy-start.1 = (f32[3,4,64,128]{3,2,1,0:T(8,128)S(1)}, f32[3,4,64,128]{3,2,1,0:T(8,128)}, u32[]{:S(2)}) copy-start(f32[3,4,64,128]{3,2,1,0:T(8,128)} %get-tuple-element.5.forward_ref) | copy-start | bytes 1179652
Sparse Core Ops, SparseCore 0:
  30.4 45.6 all-gather.7
  78.3 84.8 all-gather.5
  226.2 72.6 reduce-scatter.1

commit v2 on v1

--- a/solution.py
+++ b/solution.py
@@ -46,7 +46,10 @@
     return stacked[:rows] + (stacked[rows : 2 * rows] + stacked[2 * rows :])
 
 
-def enter(peers, me):
+LAYERS = 4
+
+
+def enter(peers, me, group=None):
     barrier = pltpu.get_barrier_semaphore()
     for offset in range(1, peers):
         pl.semaphore_signal(
@@ -55,7 +58,133 @@
             device_id={"row": lax.rem(me + offset, peers)},
             device_id_type=MESH,
         )
-    pl.semaphore_wait(barrier, peers - 1)
+    expected = peers - 1
+    if group is not None:
+        level, lane, lanes = group
+        cols = LAYERS * lanes
+        for offset in range(1, cols):
+            pl.semaphore_signal(
+                barrier,
+                inc=1,
+                device_id={"col": lax.rem(level * lanes + lane + offset, cols)},
+                device_id_type=MESH,
+            )
+        expected = expected + cols - 1
+    pl.semaphore_wait(barrier, expected)
+
+
+def has_level(level):
+    return jnp.logical_and(level >= 0, level < LAYERS)
+
+
+class Relay:
+    def __init__(self, tiles, chunks, group, send_sems, recv_sems):
+        self.tiles, self.chunks, self.group = tiles, chunks, group
+        self.send_sems, self.recv_sems = send_sems, recv_sems
+        self.sent = []
+        self.time = 0
+
+    def copy(self, chunk, owner, way, dest):
+        first, length, _ = self.chunks[chunk]
+        part = self.tiles.at[owner, pl.ds(first, length)]
+        return pltpu.make_async_remote_copy(
+            src_ref=part,
+            dst_ref=part,
+            send_sem=self.send_sems.at[chunk, owner, way],
+            recv_sem=self.recv_sems.at[chunk, owner],
+            device_id={"col": dest},
+            device_id_type=MESH,
+        )
+
+    def along(self, chunk, level, lane, way):
+        mine, my_lane, lanes = self.group
+        ok = jnp.logical_and(has_level(level), has_level(mine + way))
+
+        def one(wait):
+            @pl.when(ok)
+            def _():
+                copy = self.copy(
+                    chunk,
+                    level * lanes + lane,
+                    0 if way > 0 else 1,
+                    (mine + way) * lanes + my_lane,
+                )
+                copy.wait_send() if wait else copy.start()
+
+        one(False)
+        self.sent.append(one)
+
+    def across(self, chunk, level):
+        mine, my_lane, lanes = self.group
+
+        def one(wait):
+            @pl.when(has_level(level))
+            def _():
+                for offset in range(1, lanes):
+                    copy = self.copy(
+                        chunk,
+                        level * lanes + my_lane,
+                        1 + offset,
+                        mine * lanes + lax.rem(my_lane + offset, lanes),
+                    )
+                    copy.wait_send() if wait else copy.start()
+
+        one(False)
+        self.sent.append(one)
+
+    def take(self, chunk, level, lane):
+        mine, my_lane, lanes = self.group
+
+        @pl.when(has_level(level))
+        def _():
+            self.copy(chunk, level * lanes + lane, 0, mine * lanes + my_lane).wait_recv()
+
+    def hop(self, chunk, hop):
+        mine, my_lane, lanes = self.group
+        lane_first = self.chunks[chunk][2]
+        others = [lax.rem(my_lane + offset, lanes) for offset in range(1, lanes)]
+        if hop == 0:
+            self.across(chunk, mine)
+            self.along(chunk, mine, my_lane, 1)
+            self.along(chunk, mine, my_lane, -1)
+            return
+        if lane_first and hop == 1:
+            for lane in others:
+                self.take(chunk, mine, lane)
+                self.along(chunk, mine, lane, 1)
+                self.along(chunk, mine, lane, -1)
+        if lane_first and hop >= 2:
+            for way in (1, -1):
+                for lane in others:
+                    level = mine - way * (hop - 1)
+                    self.take(chunk, level, lane)
+                    self.along(chunk, level, lane, way)
+        if hop < LAYERS:
+            for way in (1, -1):
+                level = mine - way * hop
+                self.take(chunk, level, my_lane)
+                self.along(chunk, level, my_lane, way)
+                if not lane_first:
+                    self.across(chunk, level)
+        if not lane_first and hop == LAYERS:
+            for distance in range(1 - LAYERS, LAYERS):
+                for lane in others:
+                    self.take(chunk, mine + distance, lane)
+
+    def pump(self):
+        for chunk in range(len(self.chunks)):
+            hop = self.time - chunk
+            if 0 <= hop <= LAYERS:
+                self.hop(chunk, hop)
+        self.time += 1
+
+    def finish(self):
+        while self.time < len(self.chunks) + LAYERS:
+            self.pump()
+
+    def settle(self):
+        for one in self.sent:
+            one(True)
 
 
 def send_all(source_of, landing, send_sems, recv_sems, step, peers, me):
@@ -90,23 +219,44 @@
     panels,
     right_ref,
     inverse_ref,
-    child_ref,
-    parent_ref,
+    tiles_in,
     choice_ref,
     slices_ref,
     whole_ref,
+    tiles_out,
     gathered,
     parts,
     arrived,
+    tiles,
     send_sems,
     recv_sems,
+    relay_send,
+    relay_recv,
+    local_sem,
 ):
     me = lax.axis_index("row")
+    lanes = tiles.shape[0] // LAYERS
+    column = lax.axis_index("col")
+    group = (column // lanes, lax.rem(column, lanes), lanes)
     pair_of, pairs = pair_table(panels)
     count = len(pairs)
     rows = right_ref.shape[3]
-    enter(peers, me)
+    children, parents, ancestors = 0, 2 * count + 2 * panels, 2 * count
+    half = panels - 1
+    chunks = [
+        (0, 2 * (count - half), False),
+        (2 * (count - half), 2 * half, True),
+        (ancestors, panels, False),
+        (ancestors + panels, panels, True),
+        (parents, count, False),
+        (parents + count, tiles.shape[1] - parents - count, False),
+    ]
+    tiles[column] = tiles_in[...]
+    enter(peers, me, group)
     started = []
+    relay = Relay(tiles, chunks, group, relay_send, relay_recv)
+    relay.pump()
+    relay.pump()
 
     def spread(step, separators):
         copies = send_all(
@@ -118,6 +268,8 @@
             peers,
             me,
         )
+        if relay.time < len(chunks) + LAYERS:
+            relay.pump()
         for copy in copies:
             copy.wait_recv()
         started.extend(copies)
@@ -131,7 +283,7 @@
         for child in range(2):
             residual = right_ref[child, panel]
             for earlier in range(panel):
-                tile = tile_of(child_ref, child * count + pair_of[panel, earlier], rows)
+                tile = tile_of(tiles, 2 * pair_of[panel, earlier] + child, rows)
                 residual = residual - product(solved[child][earlier], tile, NN)
             gathered[panel, me, child] = residual
         whole = spread(panel, 2)
@@ -141,10 +293,13 @@
             for peer in range(peers):
                 parts[peer, :, 0:rows] = value[:, peer * rows : (peer + 1) * rows]
             slices_ref[child, panel] = parts[me, :, 0:rows]
+        if panel == 0:
+            relay.pump()
+            relay.pump()
     updates = []
     for child in range(2):
         for panel in range(panels):
-            tile = tile_of(child_ref, 2 * count + child * panels + panel, child_ref.shape[3])
+            tile = tile_of(tiles, ancestors + 2 * panel + child, tiles.shape[3])
             updates.append(product(solved[child][panel], tile, NN))
     update = selected(jnp.concatenate(updates, axis=1), choice_ref[...], NN)
     width = peers * rows
@@ -156,6 +311,7 @@
     copies = send_all(
         lambda dest: parts.at[dest], arrived.at[me], send_sems, recv_sems, step, peers, me
     )
+    relay.pump()
     for copy in copies:
         copy.wait_recv()
     started.extend(copies)
@@ -166,19 +322,24 @@
     for panel in range(panels):
         residual = right_ref[2, panel] - ancestor[:, panel * rows : (panel + 1) * rows]
         for earlier in range(panel):
-            tile = tile_of(parent_ref, pair_of[panel, earlier], rows)
+            tile = tile_of(tiles, parents + pair_of[panel, earlier], rows)
             residual = residual - product(solved[earlier], tile, NN)
         gathered[panels + panel, me, 0] = residual
         whole = spread(panels + panel, 1)
         value = product(whole[0], inverse_ref[2, panel], NT)
         solved.append(value)
         whole_ref[panel] = value
+    relay.finish()
+    keep = pltpu.make_async_copy(tiles, tiles_out, local_sem)
+    keep.start()
     for copy in started:
         copy.wait_send()
+    relay.settle()
     for panel in range(panels):
         for peer in range(peers):
             parts[peer, :, 0:rows] = solved[panel][:, peer * rows : (peer + 1) * rows]
         slices_ref[2, panel] = parts[me, :, 0:rows]
+    keep.wait()
 
 
 def backward_kernel(
@@ -186,10 +347,8 @@
     panels,
     forward_ref,
     inverse_ref,
-    child_ref,
-    parent_ref,
+    tiles_ref,
     choice_ref,
-    far_ref,
     slices_ref,
     gathered,
     parts,
@@ -202,8 +361,15 @@
     pair_of, pairs = pair_table(panels)
     count = len(pairs)
     rows = forward_ref.shape[3]
+    parents, ancestors = 2 * count + 2 * panels, 2 * count
+    columns = forward_ref.shape[2]
     enter(peers, me)
     started = []
+    far_parts = []
+    for index in range(parents + count, tiles_ref.shape[1]):
+        turned = tile_of(tiles_ref, index, tiles_ref.shape[3]).T
+        for begin in range(0, turned.shape[0], columns):
+            far_parts.append(turned[begin : begin + columns])
 
     def summed(step, forward, partials):
         separators = len(partials)
@@ -252,9 +418,9 @@
     solved = [None] * panels
     own = [None] * panels
     for panel in reversed(range(panels)):
-        partial = far_ref[panel]
+        partial = far_parts[panel]
         for later in range(panel + 1, panels):
-            tile = tile_of(parent_ref, pair_of[later, panel], rows)
+            tile = tile_of(tiles_ref, parents + pair_of[later, panel], rows)
             partial = partial + product(own[later], tile, NT)
         step = panels - 1 - panel
         whole = summed(step, [forward_ref[2, panel]], [partial])
@@ -268,10 +434,10 @@
         partials = []
         for child in range(2):
             place = child * panels + panel
-            tile = tile_of(child_ref, 2 * count + place, slots)
+            tile = tile_of(tiles_ref, ancestors + 2 * panel + child, slots)
             partial = product(picked[:, place * slots : (place + 1) * slots], tile, NT)
             for later in range(panel + 1, panels):
-                tile = tile_of(child_ref, child * count + pair_of[later, panel], rows)
+                tile = tile_of(tiles_ref, 2 * pair_of[later, panel] + child, rows)
                 partial = partial + product(own[child][later], tile, NT)
             partials.append(partial)
         step = 2 * panels - 1 - panel
@@ -313,46 +479,56 @@
         ]
         return tiles
 
-    anc_tiles = anc_values.transpose(0, 1, 3, 2).reshape(2 * panels, col_width, slots)
-    child_tiles = jnp.stack(lower(0) + lower(1))
-    parent_tiles = jnp.stack(lower(2))
+    anc_tiles = anc_values.transpose(1, 0, 3, 2).reshape(2 * panels, col_width, slots)
+    children = [tile for pair in zip(lower(0), lower(1)) for tile in pair]
+    block_tiles = [jnp.stack(children), jnp.stack(lower(2))]
     if rows < slots:
-        child_tiles = jnp.pad(child_tiles, ((0, 0), (0, 0), (0, slots - rows)))
-    child_all = lax.all_gather(jnp.concatenate([child_tiles, anc_tiles]), "col")
-    parent_all = lax.all_gather(parent_tiles, "col")
+        block_tiles = [
+            jnp.pad(tiles, ((0, 0), (0, 0), (0, slots - rows))) for tiles in block_tiles
+        ]
+    beside = slots // columns
+    far_back = jnp.einsum(
+        "pjr,rk->pjk", far_factor, far_solution, precision=lax.Precision.HIGH
+    )
+    far_tiles = (
+        far_back.reshape(panels // beside, beside, col_width, columns)
+        .transpose(0, 2, 1, 3)
+        .reshape(panels // beside, col_width, slots)
+    )
+    tiles = jnp.concatenate([block_tiles[0], anc_tiles, block_tiles[1], far_tiles])
+    cols = width // col_width
 
     position = lax.axis_index("row") * slots + jnp.arange(slots)
     live = position[None, None, :] < anc_count[:, :, None]
     wanted = jnp.where(live, anc_rows, -1).reshape(-1)
     choice = (wanted[:, None] == jnp.arange(panels * width)[None, :]).astype(jnp.bfloat16)
 
-    far_back = jnp.einsum(
-        "rk,pjr->pkj", far_solution, far_factor, precision=lax.Precision.HIGH
-    )
-    far_all = lax.all_gather(far_back, "col", axis=0)
-    far_whole = far_all.transpose(1, 2, 0, 3).reshape(panels, columns, width)
-
     right_turned = right_sides.transpose(0, 1, 3, 2)
-    slices, whole = pl.pallas_call(
+    slices, whole, tiles_all = pl.pallas_call(
         functools.partial(forward_kernel, peers, panels),
         out_shape=(
             jax.ShapeDtypeStruct((3, panels, columns, rows), jnp.float32),
             jax.ShapeDtypeStruct((panels, columns, width), jnp.float32),
+            jax.ShapeDtypeStruct((cols,) + tiles.shape, jnp.float32),
         ),
-        in_specs=[vmem] * 5,
-        out_specs=(vmem, vmem),
+        in_specs=[vmem] * 4,
+        out_specs=(vmem, vmem, pl.BlockSpec(memory_space=pl.ANY)),
         scratch_shapes=[
             pltpu.VMEM((2 * panels, peers, 2, columns, rows), jnp.float32),
             pltpu.VMEM((peers, columns, panels * rows), jnp.float32),
             pltpu.VMEM((peers, columns, panels * rows), jnp.float32),
+            pltpu.VMEM((cols,) + tiles.shape, jnp.float32),
             pltpu.SemaphoreType.DMA((2 * panels + 1, peers)),
             pltpu.SemaphoreType.DMA((2 * panels + 1, peers)),
+            pltpu.SemaphoreType.DMA((6, cols, 1 + cols // LAYERS)),
+            pltpu.SemaphoreType.DMA((6, cols)),
+            pltpu.SemaphoreType.DMA,
         ],
         compiler_params=pltpu.CompilerParams(
             collective_id=0, has_side_effects=True, vmem_limit_bytes=VMEM_LIMIT
         ),
         name="forward",
-    )(right_turned, diag_inverse, child_all, parent_all, choice)
+    )(right_turned, diag_inverse, tiles, choice)
 
     start = lax.axis_index("col") * col_width
     parent_cols = lax.dynamic_slice_in_dim(whole, start, col_width, 2)
@@ -366,7 +542,7 @@
     turned = pl.pallas_call(
         functools.partial(backward_kernel, peers, panels),
         out_shape=jax.ShapeDtypeStruct((3, panels, columns, rows), jnp.float32),
-        in_specs=[vmem] * 6,
+        in_specs=[vmem] * 4,
         out_specs=vmem,
         scratch_shapes=[
             pltpu.VMEM((2 * panels, peers, 2, columns, rows), jnp.float32),
@@ -380,7 +556,7 @@
             collective_id=1, has_side_effects=True, vmem_limit_bytes=VMEM_LIMIT
         ),
         name="backward",
-    )(slices, diag_inverse, child_all, parent_all, choice, far_whole)
+    )(slices, diag_inverse, tiles_all, choice)
     return (slices.transpose(0, 1, 3, 2), turned.transpose(0, 1, 3, 2), far_update)
 
 

time: 361 us -> 267 us (0.74)
  waiting for transfers between devices: 128 us -> 0.04 us
  Pallas kernels: 140 us -> 203 us
  blocking collectives: 30.6 us -> 0 us
  other arithmetic: 13.8 us -> 18.3 us
    all_gather x2 -> x0, waiting for transfers between devices: 128 us -> none  [the longest x1 87 us: on_device(): child_all = lax.all_gather(jnp.concatenate([child_tiles, anc_tiles]), 'col')]
    pallas_call x1, Pallas kernels: 55.2 us -> 123 us  [on_device(): pl.pallas_call(functools.partial(forward_kernel, peers, panels), out_shap...]
    all_gather x1 -> x0, blocking collectives: 30.6 us -> none  [on_device(): far_all = lax.all_gather(far_back, 'col', axis=0)]
    unnamed x11 -> x18, other arithmetic: 8.48 us -> 13.7 us
    pallas_call x1, Pallas kernels: 84.3 us -> 79.8 us  [on_device(): pl.pallas_call(functools.partial(backward_kernel, peers, panels), out_sha...]
  transfers between devices with their start and end apart: 3 -> 1, of which waited for: 2 -> 0; matrix products, arithmetic and copies ran while one was open for 3% -> 0% of each run, Pallas kernels for 23% -> 30%
where the time goes in v2:
time: 267 us; the launch traced here: 265 us
  Pallas kernels  203 us (76%)
  between operations  25.5 us (10%)
  other arithmetic  18.3 us (7%)
  matrix products  13.6 us (5%)
  local copies, waits for them, and re-layouts  5.42 us (2%)
    pallas_call x1, Pallas kernels, on_device(): pl.pallas_call(functools.partial(forward_kernel, peers, panels), out_shap...  123 us
    pallas_call x1, Pallas kernels, on_device(): pl.pallas_call(functools.partial(backward_kernel, peers, panels), out_sha...  79.8 us
    unnamed x18, other arithmetic  13.7 us
    dot_general x1, matrix products, on_device(): jnp.einsum('pjr,pkj->rk', far_factor, parent_cols, precision=lax.Precisio...  7.74 us
    dot_general x1, matrix products, on_device(): jnp.einsum('pjr,rk->pjk', far_factor, far_solution, precision=lax.Precisi...  5.86 us
  transfers between devices with their start and end apart: 1, of which 0 were waited for; matrix products, arithmetic and copies ran while one was open for 0% of the time, Pallas kernels for 30%

profile of v2, /device:TPU:1, one launch (start us, length us, event | category | flops | bytes accessed | tf_op | source)
XLA Modules:
  0.0 265.4 jit_solution(9965245873652077730)
XLA Ops:
  7.2 0.0 copy-start
  7.2 0.0 reduce-scatter.2.cloned.1.call-start
  7.2 1.7 fusion.5
  20.2 0.0 copy-done
  20.2 0.0 copy-start.4
  20.2 0.0 copy-start.5
  20.2 0.0 copy-start.6
  20.2 5.9 %fusion.1 = f32[4,64,64]{2,1,0:T(8,128)S(1)} fusion(f32[4,64,8192]{2,1,0:T(8,128)} %param.17, f32[8192,64]{0,1:T(8,128)S(1)} %copy-done), kind=kOutput, calls=%fused_computation.3 | convolution fusion | flops 805306368 | bytes 10551296 | tf_op jit(solution)/shard_map/pjr,rk->pjk/dot_general | solution.py:490
  26.1 0.1 copy.16
  26.2 0.1 reshape.113
  26.3 0.0 copy-done.4
  26.4 0.0 copy-done.5
  26.4 0.0 copy-done.6
  26.4 0.1 compare_select_fusion
  26.5 2.8 %fusion.choice_ref = bf16[1024,2048]{1,0:T(8,128)(2,1)} fusion(s32[1024]{0:T(1024)S(1)} %bitcast.152), kind=kLoop, calls=%fused_computation.2 | loop fusion | flops 4194304 | bytes 4198400 | tf_op jit(solution)/shard_map/convert_element_type | solution.py:504
  29.3 0.8 constant_dynamic-update-slice_fusion.19
  30.0 0.8 constant_dynamic-update-slice_fusion.18
  30.8 0.8 constant_dynamic-update-slice_fusion.17
  31.6 0.8 constant_dynamic-update-slice_fusion.16
  32.3 0.8 constant_dynamic-update-slice_fusion.15
  33.1 0.8 constant_dynamic-update-slice_fusion.14
  33.9 0.8 constant_dynamic-update-slice_fusion.13
  34.6 0.8 constant_dynamic-update-slice_fusion.12
  35.4 0.8 constant_dynamic-update-slice_fusion.11
  36.2 0.8 constant_dynamic-update-slice_fusion.10
  36.9 0.8 constant_dynamic-update-slice_fusion.9
  37.7 0.8 constant_dynamic-update-slice_fusion.8
  38.5 0.8 constant_dynamic-update-slice_fusion.6
  39.2 0.8 constant_dynamic-update-slice_fusion.5
  40.0 0.8 constant_dynamic-update-slice_fusion.4
  40.8 0.8 constant_dynamic-update-slice_fusion.3
  41.5 0.8 constant_dynamic-update-slice_fusion.2
  42.3 0.8 constant_dynamic-update-slice_fusion.1
  43.0 0.0 copy-start.2
  43.1 0.9 copy-done.2
  44.0 122.7 %forward.1 = (f32[3,4,64,128]{3,2,1,0:T(8,128)}, f32[4,64,512]{2,1,0:T(8,128)}, f32[8,28,64,128]{3,2,1,0:T(8,128)}) custom-call(f32[3,4,64,128]{3,2,1,0:T(8,128)} %bitcast.150, f32[3,4,512,512]{3,2,1,0:T(8,128)} %inverse_ref.3, f32[28,64,128]{2,1,0:T(8,128)} %copy-done.2, bf16[1024,2048]{1,0:T(8,128)(2,1)} %fusion.choice_ref), custom_call_target="tpu_custom_call" | custom-call | tf_op jit(solution)/shard_map/forward/pallas_call | solution.py:507
  166.7 7.7 %convolution_bitcast_fusion = f32[8192,64]{0,1:T(8,128)} fusion(f32[4,64,8192]{2,1,0:T(8,128)} %param.17, f32[4,64,512]{2,1,0:T(8,128)} %get-tuple-element.8, s32[]{:T(128)S(6)} %select_n.226), kind=kOutput, calls=%fused_computation | convolution fusion | flops 805306368 | bytes 10616836 | tf_op jit(solution)/shard_map/pjr,pkj->rk/dot_general | solution.py:536
  174.5 0.0 reduce-scatter.2.cloned.1.call-update
  174.5 0.0 copy-start.3
  174.5 0.0 copy-start.1
  174.5 79.8 %backward.1 = f32[3,4,64,128]{3,2,1,0:T(8,128)} custom-call(f32[3,4,64,128]{3,2,1,0:T(8,128)} %get-tuple-element.6.forward_ref, f32[3,4,512,512]{3,2,1,0:T(8,128)} %inverse_ref.3, f32[8,28,64,128]{3,2,1,0:T(8,128)} %get-tuple-element.7.tiles_ref, bf16[1024,2048]{1,0:T(8,128)(2,1)} %fusion.choice_ref), custom_call_target="tpu_custom_call" | custom-call | tf_op jit(solution)/shard_map/backward/pallas_call | solution.py:542
  254.3 0.0 reduce-scatter.2.cloned.1.call-done
  254.4 0.0 copy-done.3
  254.4 1.7 sub.3
  256.1 0.0 copy-done.1
  256.1 0.7 copy.38
  256.8 1.8 copy.39
  (4 shorter events, 0.0 us)
Async XLA Ops:
  7.2 13.0 %copy-start = (f32[8192,64]{0,1:T(8,128)S(1)}, f32[8192,64]{0,1:T(8,128)}, u32[]{:S(2)}) copy-start(f32[8192,64]{0,1:T(8,128)} %param.19) | copy-start | bytes 6291460
  7.2 247.2 %reduce-scatter.2.cloned.1.call-start = ((), (), s32[]{:S(2)}) async-start(), calls=%async_computation.1 | async-start | bytes 2359296 | tf_op jit(solution)/shard_map/reduce_scatter | solution.py:535
  20.2 6.2 %copy-start.4 = (f32[2,4,128,64]{2,3,1,0:T(8,128)S(1)}, f32[2,4,128,64]{2,3,1,0:T(8,128)}, u32[]{:S(2)}) copy-start(f32[2,4,128,64]{2,3,1,0:T(8,128)} %param.14) | copy-start | bytes 786436
  20.2 6.2 %copy-start.5 = (s32[2,4,128]{2,1,0:T(4,128)S(1)}, s32[2,4,128]{2,1,0:T(4,128)}, u32[]{:S(2)}) copy-start(s32[2,4,128]{2,1,0:T(4,128)} %param.15) | copy-start | bytes 12292
  20.2 6.2 %copy-start.6 = (s32[2,4]{1,0:T(2,128)S(1)}, s32[2,4]{1,0:T(2,128)}, u32[]{:S(2)}) copy-start(s32[2,4]{1,0:T(2,128)} %param.16) | copy-start | bytes 100
  43.0 0.9 copy-start.2
  174.5 79.9 %copy-start.3 = (f32[1024,64]{0,1:T(8,128)S(1)}, f32[1024,64]{0,1:T(8,128)}, u32[]{:S(2)}) copy-start(f32[1024,64]{0,1:T(8,128)} %param.18) | copy-start | bytes 786436
  174.5 81.6 %copy-start.1 = (f32[3,4,64,128]{3,2,1,0:T(8,128)S(1)}, f32[3,4,64,128]{3,2,1,0:T(8,128)}, u32[]{:S(2)}) copy-start(f32[3,4,64,128]{3,2,1,0:T(8,128)} %get-tuple-element.6.forward_ref) | copy-start | bytes 1179652
Sparse Core Ops, SparseCore 0:
  174.6 64.8 reduce-scatter.1

commit v3 on v2

--- a/solution.py
+++ b/solution.py
@@ -19,18 +19,17 @@
     return high, low
 
 
+def split_product(left, right, dims):
+    rows = left[0].shape[0]
+    both = lax.dot_general(
+        jnp.concatenate(left, axis=0), right[0], dims, preferred_element_type=jnp.float32
+    )
+    cross = lax.dot_general(left[0], right[1], dims, preferred_element_type=jnp.float32)
+    return both[:rows] + (both[rows:] + cross)
+
+
 def product(left, right, dims):
-    left_high, left_low = halves(left)
-    right_high, right_low = halves(right)
-    rows = left.shape[0]
-    both = lax.dot_general(
-        jnp.concatenate([left_high, left_low], axis=0),
-        right_high,
-        dims,
-        preferred_element_type=jnp.float32,
-    )
-    cross = lax.dot_general(left_high, right_low, dims, preferred_element_type=jnp.float32)
-    return both[:rows] + (both[rows:] + cross)
+    return split_product(halves(left), halves(right), dims)
 
 
 def selected(left, choice, dims):
@@ -219,7 +218,10 @@
     panels,
     right_ref,
     inverse_ref,
-    tiles_in,
+    mask_ref,
+    block_ref,
+    anc_ref,
+    far_ref,
     choice_ref,
     slices_ref,
     whole_ref,
@@ -245,20 +247,37 @@
     half = panels - 1
     chunks = [
         (0, 2 * (count - half), False),
-        (2 * (count - half), 2 * half, True),
+        (2 * (count - half), 2 * half, False),
         (ancestors, panels, False),
-        (ancestors + panels, panels, True),
+        (ancestors + panels, panels, False),
         (parents, count, False),
         (parents + count, tiles.shape[1] - parents - count, False),
     ]
-    tiles[column] = tiles_in[...]
+    beyond = tiles.shape[3] - rows
+
+    def place(index, separator, later, earlier):
+        tile = block_ref[separator, later, earlier]
+        tile = jnp.where(mask_ref[separator, later, earlier] == 1, tile, 0.0)
+        if beyond:
+            tile = jnp.concatenate([tile, jnp.zeros((tile.shape[0], beyond), tile.dtype)], axis=1)
+        tiles[column, index] = tile
+
+    for index, (later, earlier) in enumerate(pairs):
+        place(2 * index, 0, later, earlier)
+        place(2 * index + 1, 1, later, earlier)
+        place(parents + index, 2, later, earlier)
+    for panel in range(panels):
+        for child in range(2):
+            tiles[column, ancestors + 2 * panel + child] = anc_ref[child, panel]
+    for index in range(far_ref.shape[0]):
+        tiles[column, parents + count + index] = far_ref[index]
     enter(peers, me, group)
     started = []
     relay = Relay(tiles, chunks, group, relay_send, relay_recv)
     relay.pump()
     relay.pump()
 
-    def spread(step, separators):
+    def spread(step, separators, meanwhile):
         copies = send_all(
             lambda dest: gathered.at[step, me, pl.ds(0, separators)],
             gathered.at[step, me, pl.ds(0, separators)],
@@ -270,25 +289,36 @@
         )
         if relay.time < len(chunks) + LAYERS:
             relay.pump()
+        ready = meanwhile()
         for copy in copies:
             copy.wait_recv()
         started.extend(copies)
-        return [
+        whole = [
             jnp.concatenate([gathered[step, peer, index] for peer in range(peers)], axis=1)
             for index in range(separators)
         ]
+        return whole, ready
 
     solved = [[], []]
+    pending = [right_ref[child, 0] for child in range(2)]
     for panel in range(panels):
         for child in range(2):
-            residual = right_ref[child, panel]
-            for earlier in range(panel):
-                tile = tile_of(tiles, 2 * pair_of[panel, earlier] + child, rows)
-                residual = residual - product(solved[child][earlier], tile, NN)
-            gathered[panel, me, child] = residual
-        whole = spread(panel, 2)
+            gathered[panel, me, child] = pending[child]
+
+        def ahead():
+            inverses = [halves(inverse_ref[child, panel]) for child in range(2)]
+            rest = [None, None]
+            if panel + 1 < panels:
+                for child in range(2):
+                    rest[child] = right_ref[child, panel + 1]
+                    for earlier in range(panel):
+                        tile = tile_of(tiles, 2 * pair_of[panel + 1, earlier] + child, rows)
+                        rest[child] = rest[child] - product(solved[child][earlier], tile, NN)
+            return inverses, rest
+
+        whole, (inverses, pending) = spread(panel, 2, ahead)
         for child in range(2):
-            value = product(whole[child], inverse_ref[child, panel], NT)
+            value = split_product(halves(whole[child]), inverses[child], NT)
             solved[child].append(value)
             for peer in range(peers):
                 parts[peer, :, 0:rows] = value[:, peer * rows : (peer + 1) * rows]
@@ -296,6 +326,10 @@
         if panel == 0:
             relay.pump()
             relay.pump()
+        if panel + 1 < panels:
+            for child in range(2):
+                tile = tile_of(tiles, 2 * pair_of[panel + 1, panel] + child, rows)
+                pending[child] = pending[child] - product(solved[child][panel], tile, NN)
     updates = []
     for child in range(2):
         for panel in range(panels):
@@ -319,16 +353,30 @@
     for offset in range(1, peers):
         ancestor = ancestor + arrived[lax.rem(me + offset, peers)]
     solved = []
+    parent_right = [
+        right_ref[2, panel] - ancestor[:, panel * rows : (panel + 1) * rows]
+        for panel in range(panels)
+    ]
+    pending = parent_right[0]
     for panel in range(panels):
-        residual = right_ref[2, panel] - ancestor[:, panel * rows : (panel + 1) * rows]
-        for earlier in range(panel):
-            tile = tile_of(tiles, parents + pair_of[panel, earlier], rows)
-            residual = residual - product(solved[earlier], tile, NN)
-        gathered[panels + panel, me, 0] = residual
-        whole = spread(panels + panel, 1)
-        value = product(whole[0], inverse_ref[2, panel], NT)
+        gathered[panels + panel, me, 0] = pending
+
+        def ahead():
+            rest = None
+            if panel + 1 < panels:
+                rest = parent_right[panel + 1]
+                for earlier in range(panel):
+                    tile = tile_of(tiles, parents + pair_of[panel + 1, earlier], rows)
+                    rest = rest - product(solved[earlier], tile, NN)
+            return halves(inverse_ref[2, panel]), rest
+
+        whole, (inverse, pending) = spread(panels + panel, 1, ahead)
+        value = split_product(halves(whole[0]), inverse, NT)
         solved.append(value)
         whole_ref[panel] = value
+        if panel + 1 < panels:
+            tile = tile_of(tiles, parents + pair_of[panel + 1, panel], rows)
+            pending = pending - product(value, tile, NN)
     relay.finish()
     keep = pltpu.make_async_copy(tiles, tiles_out, local_sem)
     keep.start()
@@ -371,7 +419,7 @@
         for begin in range(0, turned.shape[0], columns):
             far_parts.append(turned[begin : begin + columns])
 
-    def summed(step, forward, partials):
+    def summed(step, forward, partials, first, second):
         separators = len(partials)
         for index in range(separators):
             for peer in range(peers):
@@ -385,6 +433,7 @@
             peers,
             me,
         )
+        early = first()
         for copy in copies:
             copy.wait_recv()
         started.extend(copies)
@@ -402,13 +451,15 @@
             peers,
             me,
         )
+        late = second()
         for copy in copies:
             copy.wait_recv()
         started.extend(copies)
-        return [
+        whole = [
             jnp.concatenate([gathered[step, peer, index] for peer in range(peers)], axis=1)
             for index in range(separators)
         ]
+        return whole, early, late
 
     def my_slice(value):
         for peer in range(peers):
@@ -417,35 +468,77 @@
 
     solved = [None] * panels
     own = [None] * panels
+    slots = choice_ref.shape[0] // (2 * panels)
+    width = peers * rows
+    pending = far_parts[panels - 1]
+    picked = None
     for panel in reversed(range(panels)):
-        partial = far_parts[panel]
-        for later in range(panel + 1, panels):
-            tile = tile_of(tiles_ref, parents + pair_of[later, panel], rows)
-            partial = partial + product(own[later], tile, NT)
+
+        def first():
+            return halves(inverse_ref[2, panel])
+
+        def second():
+            rest, pick = None, picked
+            if panel > 0:
+                rest = far_parts[panel - 1]
+                for later in range(panel + 1, panels):
+                    tile = tile_of(tiles_ref, parents + pair_of[later, panel - 1], rows)
+                    rest = rest + product(own[later], tile, NT)
+            if panel + 1 < panels:
+                pick = pick_from(panel + 1, pick)
+            return rest, pick
+
+        def pick_from(source, pick):
+            chosen = choice_ref[:, source * width : (source + 1) * width]
+            more = selected(solved[source], chosen, NT)
+            return more if pick is None else pick + more
+
         step = panels - 1 - panel
-        whole = summed(step, [forward_ref[2, panel]], [partial])
-        solved[panel] = product(whole[0], inverse_ref[2, panel], NN)
+        whole, inverse, (rest, picked) = summed(
+            step, [forward_ref[2, panel]], [pending], first, second
+        )
+        solved[panel] = split_product(halves(whole[0]), inverse, NN)
         own[panel] = my_slice(solved[panel])
         slices_ref[2, panel] = own[panel]
-    picked = selected(jnp.concatenate(solved, axis=1), choice_ref[...], NT)
-    slots = choice_ref.shape[0] // (2 * panels)
+        if panel > 0:
+            tile = tile_of(tiles_ref, parents + pair_of[panel, panel - 1], rows)
+            pending = rest + product(own[panel], tile, NT)
+    picked = pick_from(0, picked)
+
+    def from_parent(child, panel):
+        place = child * panels + panel
+        tile = tile_of(tiles_ref, ancestors + 2 * panel + child, slots)
+        return product(picked[:, place * slots : (place + 1) * slots], tile, NT)
+
     own = [[None] * panels, [None] * panels]
+    pending = [from_parent(child, panels - 1) for child in range(2)]
     for panel in reversed(range(panels)):
-        partials = []
+
+        def first():
+            return [halves(inverse_ref[child, panel]) for child in range(2)]
+
+        def second():
+            rest = [None, None]
+            if panel > 0:
+                for child in range(2):
+                    rest[child] = from_parent(child, panel - 1)
+                    for later in range(panel + 1, panels):
+                        tile = tile_of(tiles_ref, 2 * pair_of[later, panel - 1] + child, rows)
+                        rest[child] = rest[child] + product(own[child][later], tile, NT)
+            return rest
+
+        step = 2 * panels - 1 - panel
+        whole, inverses, rest = summed(
+            step, [forward_ref[child, panel] for child in range(2)], pending, first, second
+        )
         for child in range(2):
-            place = child * panels + panel
-            tile = tile_of(tiles_ref, ancestors + 2 * panel + child, slots)
-            partial = product(picked[:, place * slots : (place + 1) * slots], tile, NT)
-            for later in range(panel + 1, panels):
-                tile = tile_of(tiles_ref, 2 * pair_of[later, panel] + child, rows)
-                partial = partial + product(own[child][later], tile, NT)
-            partials.append(partial)
-        step = 2 * panels - 1 - panel
-        whole = summed(step, [forward_ref[child, panel] for child in range(2)], partials)
-        for child in range(2):
-            value = product(whole[child], inverse_ref[child, panel], NN)
+            value = split_product(halves(whole[child]), inverses[child], NN)
             own[child][panel] = my_slice(value)
             slices_ref[child, panel] = own[child][panel]
+        if panel > 0:
+            for child in range(2):
+                tile = tile_of(tiles_ref, 2 * pair_of[panel, panel - 1] + child, rows)
+                pending[child] = rest[child] + product(own[child][panel], tile, NT)
     for copy in started:
         copy.wait_send()
 
@@ -472,20 +565,6 @@
     _, pairs = pair_table(panels)
     vmem = pl.BlockSpec(memory_space=pltpu.VMEM)
 
-    def lower(separator):
-        tiles = [
-            jnp.where(block_mask[separator, later, earlier] == 1, sub_blocks[separator, later, earlier], 0.0).T
-            for later, earlier in pairs
-        ]
-        return tiles
-
-    anc_tiles = anc_values.transpose(1, 0, 3, 2).reshape(2 * panels, col_width, slots)
-    children = [tile for pair in zip(lower(0), lower(1)) for tile in pair]
-    block_tiles = [jnp.stack(children), jnp.stack(lower(2))]
-    if rows < slots:
-        block_tiles = [
-            jnp.pad(tiles, ((0, 0), (0, 0), (0, slots - rows))) for tiles in block_tiles
-        ]
     beside = slots // columns
     far_back = jnp.einsum(
         "pjr,rk->pjk", far_factor, far_solution, precision=lax.Precision.HIGH
@@ -495,7 +574,8 @@
         .transpose(0, 2, 1, 3)
         .reshape(panels // beside, col_width, slots)
     )
-    tiles = jnp.concatenate([block_tiles[0], anc_tiles, block_tiles[1], far_tiles])
+    total = 3 * len(pairs) + 2 * panels + far_tiles.shape[0]
+    tiles = jax.ShapeDtypeStruct((total, col_width, slots), jnp.float32)
     cols = width // col_width
 
     position = lax.axis_index("row") * slots + jnp.arange(slots)
@@ -511,7 +591,7 @@
             jax.ShapeDtypeStruct((panels, columns, width), jnp.float32),
             jax.ShapeDtypeStruct((cols,) + tiles.shape, jnp.float32),
         ),
-        in_specs=[vmem] * 4,
+        in_specs=[vmem, vmem, pl.BlockSpec(memory_space=pltpu.SMEM)] + [vmem] * 4,
         out_specs=(vmem, vmem, pl.BlockSpec(memory_space=pl.ANY)),
         scratch_shapes=[
             pltpu.VMEM((2 * panels, peers, 2, columns, rows), jnp.float32),
@@ -528,7 +608,15 @@
             collective_id=0, has_side_effects=True, vmem_limit_bytes=VMEM_LIMIT
         ),
         name="forward",
-    )(right_turned, diag_inverse, tiles, choice)
+    )(
+        right_turned,
+        diag_inverse,
+        block_mask,
+        sub_blocks.transpose(0, 1, 2, 4, 3),
+        anc_values.transpose(0, 1, 3, 2),
+        far_tiles,
+        choice,
+    )
 
     start = lax.axis_index("col") * col_width
     parent_cols = lax.dynamic_slice_in_dim(whole, start, col_width, 2)

time: 267 us -> 227 us (0.85)
  Pallas kernels: 203 us -> 189 us
  other arithmetic: 18.3 us -> 4.46 us
  between operations: 25.5 us -> 14.1 us
    unnamed x18 -> x0, other arithmetic: 13.7 us -> none
    pallas_call x1, Pallas kernels: 123 us -> 112 us  [on_device(): pl.pallas_call(functools.partial(forward_kernel, peers, panels), out_shap...]
    pallas_call x1, Pallas kernels: 79.8 us -> 76.7 us  [on_device(): pl.pallas_call(functools.partial(backward_kernel, peers, panels), out_sha...]
  transfers between devices with their start and end apart: 1 -> 1, of which waited for: 0 -> 0; matrix products, arithmetic and copies ran while one was open for 0% -> 0% of each run, Pallas kernels for 30% -> 34%
where the time goes in v3:
time: 227 us
  Pallas kernels  189 us (83%)
  between operations  14.1 us (6%)
  matrix products  13.7 us (6%)
  local copies, waits for them, and re-layouts  4.9 us (2%)
  other arithmetic  4.46 us (2%)
    pallas_call x1, Pallas kernels, on_device(): pl.pallas_call(functools.partial(forward_kernel, peers, panels), out_shap...  112 us
    pallas_call x1, Pallas kernels, on_device(): pl.pallas_call(functools.partial(backward_kernel, peers, panels), out_sha...  76.7 us
    dot_general x1, matrix products, on_device(): jnp.einsum('pjr,pkj->rk', far_factor, parent_cols, precision=lax.Precisio...  7.89 us
    dot_general x1, matrix products, on_device(): jnp.einsum('pjr,rk->pjk', far_factor, far_solution, precision=lax.Precisi...  5.81 us
  transfers between devices with their start and end apart: 1, of which 0 were waited for; matrix products, arithmetic and copies ran while one was open for 0% of the time, Pallas kernels for 34%

profile of v3, /device:TPU:1, one launch (start us, length us, event | category | flops | bytes accessed | tf_op | source)
XLA Modules:
  0.0 226.5 jit_solution(10597660433217411871)
XLA Ops:
  7.2 0.0 copy-start
  7.2 0.0 copy-start.4
  7.2 0.0 copy-start.3
  7.2 0.0 reduce-scatter.2.cloned.1.call-start
  7.3 1.5 copy-done
  8.8 5.8 %fusion.1 = f32[4,64,64]{2,1,0:T(8,128)S(1)} fusion(f32[4,64,8192]{2,1,0:T(8,128)} %param.17, f32[8192,64]{0,1:T(8,128)S(1)} %copy-done), kind=kOutput, calls=%fused_computation.3 | convolution fusion | flops 805306368 | bytes 10551296 | tf_op jit(solution)/shard_map/pjr,rk->pjk/dot_general | solution.py:569
  14.6 0.1 copy.15
  14.7 0.8 reshape.19.far_ref
  15.5 0.0 copy-done.4
  15.5 0.0 copy-done.3
  15.5 0.1 compare_select_fusion
  15.5 2.7 %fusion.choice_ref = bf16[1024,2048]{1,0:T(8,128)(2,1)} fusion(s32[1024]{0:T(1024)S(1)} %bitcast.26), kind=kLoop, calls=%fused_computation.2 | loop fusion | flops 4194304 | bytes 4198400 | tf_op jit(solution)/shard_map/convert_element_type | solution.py:584
  18.2 112.5 %forward.1 = (f32[3,4,64,128]{3,2,1,0:T(8,128)}, f32[4,64,512]{2,1,0:T(8,128)}, f32[8,28,64,128]{3,2,1,0:T(8,128)}) custom-call(f32[3,4,64,128]{3,2,1,0:T(8,128)} %bitcast.24, f32[3,4,512,512]{3,2,1,0:T(8,128)} %inverse_ref.3, s32[3,4,4]{2,1,0:T(4,128)} %mask_ref.1, f32[3,4,4,64,128]{4,3,2,1,0:T(8,128)} %bitcast.21, f32[2,4,64,128]{3,2,1,0:T(8,128)} %bitcast.25, ...), custom_call_target="tpu_custom_call" | custom-call | tf_op jit(solution)/shard_map/forward/pallas_call | solution.py:587
  130.7 7.9 %convolution_bitcast_fusion = f32[8192,64]{0,1:T(8,128)} fusion(f32[4,64,8192]{2,1,0:T(8,128)} %param.17, f32[4,64,512]{2,1,0:T(8,128)} %get-tuple-element.8, s32[]{:T(128)S(6)} %select_n.8), kind=kOutput, calls=%fused_computation | convolution fusion | flops 805306368 | bytes 10616836 | tf_op jit(solution)/shard_map/pjr,pkj->rk/dot_general | solution.py:624
  138.6 0.0 reduce-scatter.2.cloned.1.call-update
  138.6 0.0 copy-start.2
  138.7 0.0 copy-start.1
  138.7 76.7 %backward.1 = f32[3,4,64,128]{3,2,1,0:T(8,128)} custom-call(f32[3,4,64,128]{3,2,1,0:T(8,128)} %get-tuple-element.6.forward_ref, f32[3,4,512,512]{3,2,1,0:T(8,128)} %inverse_ref.3, f32[8,28,64,128]{3,2,1,0:T(8,128)} %get-tuple-element.7.tiles_ref, bf16[1024,2048]{1,0:T(8,128)(2,1)} %fusion.choice_ref), custom_call_target="tpu_custom_call" | custom-call | tf_op jit(solution)/shard_map/backward/pallas_call | solution.py:630
  215.4 0.0 reduce-scatter.2.cloned.1.call-done
  215.4 0.0 copy-done.2
  215.5 1.7 sub.3
  217.1 0.0 copy-done.1
  217.1 0.7 copy.18
  217.9 1.8 copy.19
  (1 shorter events, 0.0 us)
Async XLA Ops:
  7.2 1.6 copy-start
  7.2 8.3 %copy-start.4 = (s32[2,4]{1,0:T(2,128)S(1)}, s32[2,4]{1,0:T(2,128)}, u32[]{:S(2)}) copy-start(s32[2,4]{1,0:T(2,128)} %param.16) | copy-start | bytes 100
  7.2 8.3 %copy-start.3 = (s32[2,4,128]{2,1,0:T(4,128)S(1)}, s32[2,4,128]{2,1,0:T(4,128)}, u32[]{:S(2)}) copy-start(s32[2,4,128]{2,1,0:T(4,128)} %param.15) | copy-start | bytes 12292
  7.2 208.2 %reduce-scatter.2.cloned.1.call-start = ((), (), s32[]{:S(2)}) async-start(), calls=%async_computation.1 | async-start | bytes 2359296 | tf_op jit(solution)/shard_map/reduce_scatter | solution.py:623
  138.6 76.8 %copy-start.2 = (f32[1024,64]{0,1:T(8,128)S(1)}, f32[1024,64]{0,1:T(8,128)}, u32[]{:S(2)}) copy-start(f32[1024,64]{0,1:T(8,128)} %param.18) | copy-start | bytes 786436
  138.7 78.5 %copy-start.1 = (f32[3,4,64,128]{3,2,1,0:T(8,128)S(1)}, f32[3,4,64,128]{3,2,1,0:T(8,128)}, u32[]{:S(2)}) copy-start(f32[3,4,64,128]{3,2,1,0:T(8,128)} %get-tuple-element.6.forward_ref) | copy-start | bytes 1179652
Sparse Core Ops, SparseCore 0:
  138.8 63.9 reduce-scatter.1
